TPU v7x, 32 devices: a whole 2x2x4 slice. The times are simulated.
32 devices in a mesh: row: 4 (over y, x), col: 8 (over z, core).
Axes of the slice: x: 2, y: 2, z: 4, core: 2. Of those that a mesh axis runs over, the one named last changes fastest.
Arguments:
- tokens: bfloat16 [16384, 1024], P(('row', 'col')), may hold values from -6 to 6
- blocks: int32 [16384], P(('row', 'col')), may hold values from 0 to 127, never falling along the last dimension, each value on 1 to 256 neighbouring positions
- w_qkv: bfloat16 [1024, 3, 1024], P('row', None, 'col'), may hold values from -0.25 to 0.25
- b_qv: bfloat16 [2, 1024], P(None, 'col'), may hold values from -1.5 to 1.5
- w_out: bfloat16 [1024, 1024], P('col', 'row'), may hold values from -0.5 to 0.5
- b_out: bfloat16 [1024], replicated, may hold values from -3 to 3
- w_up: bfloat16 [4096, 1024], P('col', 'row'), may hold values from -0.1875 to 0.1875
- b_up: bfloat16 [4096], P('col'), may hold values from -3 to 3
- w_down: bfloat16 [4096, 1024], P('col', 'row'), may hold values from -0.09375 to 0.09375
- b_down: bfloat16 [1024], replicated, may hold values from -3 to 3
- gain1: bfloat16 [1024], replicated, may hold values from 0.5 to 1.5
- shift1: bfloat16 [1024], replicated, may hold values from -1.5 to 1.5
- gain2: bfloat16 [1024], replicated, may hold values from 0.5 to 1.5
- shift2: bfloat16 [1024], replicated, may hold values from -1.5 to 1.5
- grad_out: bfloat16 [16384, 1024], P(('row', 'col')), may hold values from -9 to 9
Outputs:
- output: bfloat16 [16384, 1024], P(('row', 'col'))
- grad_tokens: float32 [16384, 1024], P(('row', 'col'))
- grad_w_qkv: float32 [1024, 3, 1024], P('row', None, 'col')
- grad_b_qv: float32 [2, 1024], P(None, 'col')
- grad_w_out: float32 [1024, 1024], P('col', 'row')
- grad_b_out: float32 [1024], replicated
- grad_w_up: float32 [4096, 1024], P('col', 'row')
- grad_b_up: float32 [4096], P('col')
- grad_w_down: float32 [4096, 1024], P('col', 'row')
- grad_b_down: float32 [1024], replicated
- grad_gain1: float32 [1024], replicated
- grad_shift1: float32 [1024], replicated
- grad_gain2: float32 [1024], replicated
- grad_shift2: float32 [1024], replicated
Inputs may be any that keep to these rules, and one draw needn't show every extreme that they name: `blocks`: block indices never fall along the tokens and every index from the least to the largest occurs; each block holds 1 to 256 tokens, and one holds exactly 256. A block may run across the end of a sequence.
All inputs are finite; a program needn't handle non-finite values.
Results may differ from a plain program's by a relative error of at most 0.012.
The roundings to bfloat16 on the way count: a program that leaves them out, or rounds other values in their place, can miss the bound.
Values may be sent and summed in bfloat16 or wider, within the bound.
A program may use at most 256 MiB of HBM per device.

v0:
```python
import jax
import jax.numpy as jnp
from jax import lax
from jax.sharding import PartitionSpec as P

HD = 64
SEQ_LEN = 4096
EPS = 1e-05


def norm(values_in, gain, shift):
    center = jnp.mean(values_in, axis=-1, keepdims=True)
    centered = values_in - center
    spread = jnp.mean(centered * centered, axis=-1, keepdims=True)
    return centered * lax.rsqrt(spread + EPS) * gain + shift


def gelu_tanh(values_in):
    return jax.nn.gelu(values_in, approximate=True)


def gather_tokens(rows_in):
    return lax.all_gather(rows_in, "col", axis=0, tiled=True)


def sum_tokens(term_fn, local_rows):
    return lax.psum_scatter(
        term_fn(jnp.int32(0), lax.axis_size("col") * local_rows),
        "col",
        scatter_dimension=0,
        tiled=True,
    )


def body(
    tokens,
    blocks,
    w_qkv,
    b_qv,
    w_out,
    b_out,
    w_up,
    b_up,
    w_down,
    b_down,
    gain1,
    shift1,
    gain2,
    shift2,
    grad_out,
):
    f32 = jnp.float32
    bf16 = jnp.bfloat16
    local_rows = tokens.shape[0]
    model_width = tokens.shape[1]
    col_count = lax.axis_size("col")
    group_rows = local_rows * col_count
    head_cols = w_qkv.shape[2]
    heads_here = head_cols // HD
    score_scale = HD ** (-0.5)
    query_rows = min(512, SEQ_LEN)
    block_count = group_rows // query_rows
    qkv_weight = lax.all_gather(w_qkv, "row", axis=0, tiled=True)
    qkv_flat = qkv_weight.reshape(model_width, 3 * head_cols)
    out_weight, down_weight, up_weight = (
        lax.all_gather(w_out, "row", axis=1, tiled=True),
        lax.all_gather(w_down, "row", axis=1, tiled=True),
        lax.all_gather(w_up, "row", axis=1, tiled=True),
    )
    tokens_f = tokens.astype(f32)
    normed_in, norm1_back = jax.vjp(norm, tokens_f, gain1.astype(f32), shift1.astype(f32))
    attn_input = normed_in.astype(bf16)
    attn_rows, block_ids = (
        lax.all_gather(attn_input, "col", axis=0, tiled=True),
        lax.all_gather(blocks, "col", axis=0, tiled=True),
    )
    bias_qv = b_qv.astype(f32)
    mixed = jnp.dot(attn_rows, qkv_flat, preferred_element_type=f32).reshape(
        group_rows, 3, head_cols
    )
    queries = (mixed[:, 0] + bias_qv[0]).astype(bf16).reshape(group_rows, heads_here, HD)
    keys = mixed[:, 1].astype(bf16).reshape(group_rows, heads_here, HD)
    values = (mixed[:, 2] + bias_qv[1]).astype(bf16).reshape(group_rows, heads_here, HD)

    def block_scores(row_start):
        seq_start = row_start // SEQ_LEN * SEQ_LEN
        query_part = lax.dynamic_slice_in_dim(queries, row_start, query_rows, 0)
        key_seq = lax.dynamic_slice_in_dim(keys, seq_start, SEQ_LEN, 0)
        query_blocks = lax.dynamic_slice_in_dim(block_ids, row_start, query_rows, 0)
        key_blocks = lax.dynamic_slice_in_dim(block_ids, seq_start, SEQ_LEN, 0)
        raw_scores = jnp.einsum("qhd,khd->hqk", query_part, key_seq, preferred_element_type=f32)
        allowed = query_blocks[:, None] >= key_blocks[None, :]
        scores = jnp.where(allowed[None], raw_scores * score_scale, -1e30)
        return (scores, query_part, key_seq, seq_start)

    def forward_block(block_index):
        row_start = block_index * query_rows
        scores, query_part, key_seq, seq_start = block_scores(row_start)
        value_seq = lax.dynamic_slice_in_dim(values, seq_start, SEQ_LEN, 0)
        row_max = jnp.max(scores, axis=-1, keepdims=True)
        row_total = jnp.sum(jnp.exp(scores - row_max), axis=-1, keepdims=True)
        log_total = row_max + jnp.log(row_total)
        probs_low = jnp.exp(scores - log_total).astype(bf16)
        block_out = jnp.einsum("hqk,khd->qhd", probs_low, value_seq, preferred_element_type=f32)
        return (block_out, log_total)

    block_outs, log_totals = lax.map(forward_block, jnp.arange(block_count, dtype=jnp.int32))
    heads_out = block_outs.reshape(group_rows, head_cols).astype(bf16)
    part = heads_out
    attn_branch = lax.psum_scatter(
        jnp.dot(part, out_weight, preferred_element_type=f32),
        "col",
        scatter_dimension=0,
        tiled=True,
    )
    resid = tokens_f + attn_branch + b_out.astype(f32)
    normed_mid, norm2_back = jax.vjp(norm, resid, gain2.astype(f32), shift2.astype(f32))
    ffn_input = normed_mid.astype(bf16)
    up_all, down_all, up_bias = (up_weight, down_weight, b_up)
    ffn_rows = gather_tokens(ffn_input)
    up_pre = jnp.einsum("td,fd->tf", ffn_rows, up_all, preferred_element_type=f32) + up_bias.astype(
        f32
    )
    hidden_f, gelu_back = jax.vjp(gelu_tanh, up_pre)
    hidden = hidden_f.astype(bf16)
    part = hidden
    ffn_branch = lax.psum_scatter(
        jnp.dot(part, down_all, preferred_element_type=f32).astype(jnp.bfloat16),
        "col",
        scatter_dimension=0,
        tiled=True,
    ).astype(jnp.float32)
    output = (resid + ffn_branch + b_down.astype(f32)).astype(bf16)
    grad_f = grad_out.astype(f32)
    grad_bdown = jnp.sum(grad_f, axis=0)
    grad_rows = gather_tokens(grad_out)
    grad_wdown = jnp.einsum("tf,td->fd", hidden, grad_rows, preferred_element_type=f32)
    d_hidden = jnp.einsum("td,fd->tf", grad_rows, down_all, preferred_element_type=f32)
    d_up = gelu_back(d_hidden)[0]
    grad_bup = jnp.sum(d_up, axis=0)
    d_up_low = d_up.astype(bf16)
    grad_wup = jnp.einsum("tf,td->fd", d_up_low, ffn_rows, preferred_element_type=f32)

    def up_term(row_start, count):
        return jnp.dot(d_up_low, up_all, preferred_element_type=f32)

    d_norm2 = sum_tokens(up_term, local_rows)
    d_resid_in, grad_gain2, grad_shift2 = norm2_back(d_norm2)
    d_resid = grad_f + d_resid_in
    grad_bout = jnp.sum(d_resid, axis=0)
    d_resid_low = d_resid.astype(bf16)
    resid_rows = gather_tokens(d_resid_low)
    grad_wout = jnp.einsum("tk,td->kd", heads_out, resid_rows, preferred_element_type=f32)
    d_heads = jnp.einsum("td,kd->tk", resid_rows, out_weight, preferred_element_type=f32).astype(
        bf16
    )
    d_heads = d_heads.reshape(group_rows, heads_here, HD)

    def backward_block(carry, block_index):
        grad_keys, grad_values = carry
        row_start = block_index * query_rows
        scores, query_part, key_seq, seq_start = block_scores(row_start)
        value_seq = lax.dynamic_slice_in_dim(values, seq_start, SEQ_LEN, 0)
        probs = jnp.exp(scores - log_totals[block_index])
        probs_low = probs.astype(bf16)
        dout_part = lax.dynamic_slice_in_dim(d_heads, row_start, query_rows, 0)
        value_part = jnp.einsum("hqk,qhd->khd", probs_low, dout_part, preferred_element_type=f32)
        d_probs = jnp.einsum("qhd,khd->hqk", dout_part, value_seq, preferred_element_type=f32)
        d_scores = probs * (d_probs - jnp.sum(probs * d_probs, axis=-1, keepdims=True))
        d_scores_low = d_scores.astype(bf16)
        query_grad = (
            jnp.einsum("hqk,khd->qhd", d_scores_low, key_seq, preferred_element_type=f32)
            * score_scale
        )
        key_part = (
            jnp.einsum("hqk,qhd->khd", d_scores_low, query_part, preferred_element_type=f32)
            * score_scale
        )
        old_keys = lax.dynamic_slice_in_dim(grad_keys, seq_start, SEQ_LEN, 0)
        grad_keys = lax.dynamic_update_slice_in_dim(grad_keys, old_keys + key_part, seq_start, 0)
        old_values = lax.dynamic_slice_in_dim(grad_values, seq_start, SEQ_LEN, 0)
        grad_values = lax.dynamic_update_slice_in_dim(
            grad_values, old_values + value_part, seq_start, 0
        )
        return ((grad_keys, grad_values), query_grad)

    empty = jnp.zeros((group_rows, heads_here, HD), f32)
    (grad_keys, grad_values), grad_queries = lax.scan(
        backward_block, (empty, empty), jnp.arange(block_count, dtype=jnp.int32)
    )
    grad_queries = grad_queries.reshape(group_rows, head_cols)
    grad_keys = grad_keys.reshape(group_rows, head_cols)
    grad_values = grad_values.reshape(group_rows, head_cols)
    grad_bqv = jnp.stack([jnp.sum(grad_queries, axis=0), jnp.sum(grad_values, axis=0)])
    d_mixed = jnp.stack([grad_queries, grad_keys, grad_values], axis=1).astype(bf16)
    d_mixed_flat = d_mixed.reshape(group_rows, 3 * head_cols)
    grad_wqkv = jnp.einsum(
        "td,tk->dk", attn_rows, d_mixed_flat, preferred_element_type=f32
    ).reshape(model_width, 3, head_cols)

    def qkv_term(row_start, count):
        return jnp.einsum("tk,dk->td", d_mixed_flat, qkv_flat, preferred_element_type=f32)

    d_norm1 = sum_tokens(qkv_term, local_rows)
    d_tokens_in, grad_gain1, grad_shift1 = norm1_back(d_norm1)
    grad_tokens = d_resid + d_tokens_in
    grad_wqkv = lax.psum_scatter(grad_wqkv, "row", scatter_dimension=0, tiled=True)
    grad_wout, grad_wdown, grad_wup = (
        lax.psum_scatter(grad_wout, "row", scatter_dimension=1, tiled=True),
        lax.psum_scatter(grad_wdown, "row", scatter_dimension=1, tiled=True),
        lax.psum_scatter(grad_wup, "row", scatter_dimension=1, tiled=True),
    )
    grad_bqv, grad_bup = lax.psum((grad_bqv, grad_bup), "row")
    grad_gain1, grad_shift1, grad_gain2, grad_shift2, grad_bout, grad_bdown = lax.psum(
        (grad_gain1, grad_shift1, grad_gain2, grad_shift2, grad_bout, grad_bdown), ("row", "col")
    )
    return (
        output,
        grad_tokens,
        grad_wqkv,
        grad_bqv,
        grad_wout,
        grad_bout,
        grad_wup,
        grad_bup,
        grad_wdown,
        grad_bdown,
        grad_gain1,
        grad_shift1,
        grad_gain2,
        grad_shift2,
    )


def solution(mesh):
    return jax.shard_map(
        body,
        mesh=mesh,
        in_specs=(
            P(("row", "col"), None),
            P(("row", "col")),
            P("row", None, "col"),
            P(None, "col"),
            P("col", "row"),
            P(),
            P("col", "row"),
            P("col"),
            P("col", "row"),
            P(),
            P(),
            P(),
            P(),
            P(),
            P(("row", "col"), None),
        ),
        out_specs=(
            P(("row", "col"), None),
            P(("row", "col"), None),
            P("row", None, "col"),
            P(None, "col"),
            P("col", "row"),
            P(),
            P("col", "row"),
            P("col"),
            P("col", "row"),
            P(),
            P(),
            P(),
            P(),
            P(),
        ),
        check_vma=False,
    )
```

profile of v0, /device:TPU:0, one launch (start us, length us, event | category | flops | bytes accessed | tf_op | source)
XLA Modules:
  0.0 1738.0 jit_solution(14940055284473691748)
XLA Ops:
  15.6 12.7 all_gather.29
  28.6 13.3 all-gather
  41.9 10.6 all_gather.30
  53.5 46.9 %all-gather.8.cloned.1.call-done = bf16[4096,1024]{1,0:T(8,128)(2,1)} async-done(((bf16[512,1024]{1,0:T(8,128)(2,1)}), bf16[4096,1024]{1,0:T(8,128)(2,1)}) %all-gather.8.cloned.1.call-update) | async-done | bytes 8388624 | tf_op jit(solution)/shard_map/all_gather | solution.py:74
  100.4 5.9 fusion.44
  107.3 127.8 %while.29 = (s32[]{:T(128)}, bf16[8,512,2,64]{1,3,2,0:T(8,128)(2,1)}, f32[8,2,512,1]{2,1,3,0:T(2,128)S(1)}, s32[8]{0:T(128)S(1)}, s32[4096]{0:T(1024)S(1)}, /*in...) while((s32[]{:T(128)}, ...), condition=%wide.region_5.6_spmd.clone, body=%wide.region_2.5_spmd.sunk.clone | while | flops 1121975296 | bytes 61266096 | solution.py:107
  238.1 8.1 fusion.77
  247.0 166.2 %reduce-scatter.9.cloned.1.call-done = f32[512,1024]{1,0:T(8,128)} async-done(((f32[4096,1024]{1,0:T(8,128)}), f32[512,1024]{1,0:T(8,128)}) %reduce-scatter.9.cloned.1.call-update) | async-done | bytes 2097168 | tf_op jit(solution)/shard_map/reduce_scatter | solution.py:110
  418.7 78.9 %all-gather.10.cloned.1.call-done = bf16[4096,1024]{1,0:T(8,128)(2,1)} async-done(((bf16[512,1024]{1,0:T(8,128)(2,1)}), bf16[4096,1024]{1,0:T(8,128)(2,1)}) %all-gather.10.cloned.1.call-update) | async-done | bytes 8388624 | tf_op jit(solution)/shard_map/all_gather | solution.py:23
  497.6 11.4 fusion.78
  509.0 15.2 all-gather.14.cloned.1.call-done
  524.1 83.6 %all-gather.16.cloned.1.call-done = bf16[4096,1024]{1,0:T(8,128)(2,1)} async-done(((bf16[512,1024]{1,0:T(8,128)(2,1)}), bf16[4096,1024]{1,0:T(8,128)(2,1)}) %all-gather.16.cloned.1.call-update) | async-done | bytes 8388624 | tf_op jit(solution)/shard_map/all_gather | solution.py:23
  607.7 14.8 fusion.71
  624.5 8.1 fusion.61
  632.9 12.6 convolution_convert_fusion
  646.1 153.2 %reduce-scatter.13.cloned.1.call-done = f32[512,1024]{1,0:T(8,128)} async-done(((f32[4096,1024]{1,0:T(8,128)}), f32[512,1024]{1,0:T(8,128)}) %reduce-scatter.13.cloned.1.call-update) | async-done | bytes 2097168 | tf_op jit(solution)/shard_map/reduce_scatter | solution.py:27
  802.2 87.3 %reduce-scatter.11.cloned.1.call-done = bf16[512,1024]{1,0:T(8,128)(2,1)} async-done(((bf16[4096,1024]{1,0:T(8,128)(2,1)}), bf16[512,1024]{1,0:T(8,128)(2,1)}) %reduce-scatter.11.cloned.1.call-update) | async-done | bytes 1048592 | tf_op jit(solution)/shard_map/reduce_scatter | solution.py:127
  896.0 80.6 %all-gather.18.cloned.1.call-done = bf16[4096,1024]{1,0:T(8,128)(2,1)} async-done(((bf16[512,1024]{1,0:T(8,128)(2,1)}), bf16[4096,1024]{1,0:T(8,128)(2,1)}) %all-gather.18.cloned.1.call-update) | async-done | bytes 8388624 | tf_op jit(solution)/shard_map/all_gather | solution.py:23
  976.6 7.2 convolution_convert_fusion.1
  983.8 418.1 %while.30 = (s32[]{:T(128)}, f32[4096,2,64]{0,2,1:T(8,128)S(1)}, f32[4096,2,64]{0,2,1:T(8,128)}, f32[8,512,2,64]{1,3,2,0:T(8,128)}, s32[8]{0:T(128)S(1)}, /*inde...) while((s32[]{:T(128)}, f32[4096,2,64]{0,2,1:T(8,128)S(1)}, ...), condition=%wide.region_15.16_spmd.clone.clone, body=%wide.region_13.15_spmd.clone.sunk.clone | while | flops 2752052224 | bytes 217893168 | solution.py:188
  992.1 5.7 copy-done
  997.8 7.2 fusion.153
  1005.0 12.7 multiply_reduce_fusion.6
  1017.7 12.3 multiply_convert_fusion.6
  1043.9 5.7 copy-done
  1049.7 7.6 fusion.153
  1057.3 12.6 multiply_reduce_fusion.6
  1069.9 12.3 multiply_convert_fusion.6
  1096.2 5.7 copy-done
  1101.9 7.6 fusion.153
  1109.5 12.7 multiply_reduce_fusion.6
  1122.2 12.3 multiply_convert_fusion.6
  1148.4 5.7 copy-done
  1154.2 7.6 fusion.153
  1161.8 12.6 multiply_reduce_fusion.6
  1174.4 12.3 multiply_convert_fusion.6
  1200.7 5.7 copy-done
  1206.4 7.6 fusion.153
  1214.0 12.6 multiply_reduce_fusion.6
  1226.7 12.3 multiply_convert_fusion.6
  1252.9 5.7 copy-done
  1258.6 7.6 fusion.153
  1266.3 12.7 multiply_reduce_fusion.6
  1278.9 12.3 multiply_convert_fusion.6
  1305.2 5.7 copy-done
  1310.9 7.6 fusion.153
  1318.5 12.7 multiply_reduce_fusion.6
  1331.2 12.3 multiply_convert_fusion.6
  1357.4 5.7 copy-done
  1363.1 7.6 fusion.153
  1370.8 12.7 multiply_reduce_fusion.6
  1383.4 12.3 multiply_convert_fusion.6
  1402.7 6.4 copy.50
  1414.9 9.3 convolution_bitcast_fusion
  1424.2 10.6 fusion.59
  1435.1 12.0 fusion.69
  1453.9 5.5 fusion.79
  1459.6 9.0 fusion.42
  1471.0 10.4 all-reduce.1
  1481.4 109.7 %reduce-scatter.15.cloned.1.call-done = f32[512,1024]{1,0:T(8,128)} async-done(((f32[4096,1024]{1,0:T(8,128)}), f32[512,1024]{1,0:T(8,128)}) %reduce-scatter.15.cloned.1.call-update) | async-done | bytes 2097168 | tf_op jit(solution)/shard_map/reduce_scatter | solution.py:27
  1596.8 38.7 %all-reduce = (f32[1024]{0:T(1024)}, f32[1024]{0:T(1024)}, f32[1024]{0:T(1024)}, f32[1024]{0:T(1024)}, f32[1024]{0:T(1024)}, /*index=5*/f32[1024]{0:T(1024)}) all-reduce(f32[1024]{0:T(1024)S(1)} %get-tuple-element.165, f32[1024]{0:T(1024)S(1)} %get-tuple-element.164, ...), channel_id=1, replica_groups=mesh['row'=4,'col'=8] {'row','col'}, use_global_device_ids=true, to_apply=%region_25.26 | all-reduce | flops 6144 | bytes 49152 | tf_op jit(solution)/shard_map/psum | solution.py:214
  1635.5 31.8 %reduce-scatter.23.cloned.1.call-done = f32[512,256]{1,0:T(8,128)} async-done(((f32[512,1024]{1,0:T(8,128)}), f32[512,256]{1,0:T(8,128)}) %reduce-scatter.23.cloned.1.call-update) | async-done | bytes 524304 | tf_op jit(solution)/shard_map/reduce_scatter | solution.py:210
  1667.4 28.2 %reduce-scatter.19.cloned.1.call-done = f32[128,256]{1,0:T(8,128)} async-done(((f32[128,1024]{1,0:T(8,128)}), f32[128,256]{1,0:T(8,128)}) %reduce-scatter.19.cloned.1.call-update) | async-done | bytes 131088 | tf_op jit(solution)/shard_map/reduce_scatter | solution.py:209
  1695.6 34.8 %reduce-scatter.17.cloned.1.call-done = f32[256,3,128]{2,0,1:T(8,128)} async-done(((f32[1024,3,128]{2,0,1:T(8,128)}), f32[256,3,128]{2,0,1:T(8,128)}) %reduce-scatter.17.cloned.1.call-update) | async-done | bytes 393232 | tf_op jit(solution)/shard_map/reduce_scatter | solution.py:207
  (296 shorter events, 265.5 us)
Async XLA Ops:
  8.0 7.4 copy-start.38
  8.0 7.6 copy-start.14
  8.0 20.5 %copy-start.28 = (s32[512]{0:T(512)S(1)}, s32[512]{0:T(512)}, u32[]{:S(2)}) copy-start(s32[512]{0:T(512)} %param.20) | copy-start | bytes 6148
  8.0 33.8 %copy-start.19 = (bf16[128,256]{1,0:T(8,128)(2,1)S(1)}, bf16[128,256]{1,0:T(8,128)(2,1)}, u32[]{:S(2)}) copy-start(bf16[128,256]{1,0:T(8,128)(2,1)} %param.23) | copy-start | bytes 196612
  8.1 92.3 %all-gather.8.cloned.1.call-start = ((), (), s32[]{:S(2)}) async-start(), calls=%async_computation.8 | async-start | bytes 9437184 | tf_op jit(solution)/shard_map/all_gather | solution.py:74
  9.6 3.1 copy-start.17
  11.3 4.3 copy-start.24
  11.3 4.3 copy-start.20
  15.3 397.9 %reduce-scatter.9.cloned.1.call-start = ((), (), s32[]{:S(2)}) async-start(), calls=%async_computation.9 | async-start | bytes 18874368 | tf_op jit(solution)/shard_map/reduce_scatter | solution.py:110
  28.3 78.0 %copy-start.12 = (bf16[1024,3,128]{2,0,1:T(8,128)(2,1)}, bf16[1024,3,128]{2,0,1:T(8,128)(2,1)S(1)}, u32[]{:S(2)}) copy-start(bf16[1024,3,128]{2,0,1:T(8,128)(2,1)S(1)} %all_gather.29) | copy-start | bytes 2359300
  235.1 2.6 copy-start.13
  235.2 11.1 copy-start.2
  238.1 8.1 copy-start.7
  246.3 0.7 copy-start.31
  246.3 172.4 %all-gather.12.cloned.1.call-start = ((), (), s32[]{:S(2)}) async-start(), calls=%async_computation.11 | async-start | bytes 1310720 | tf_op jit(solution)/shard_map/all_gather | solution.py:68
  246.9 250.7 %all-gather.10.cloned.1.call-start = ((), (), s32[]{:S(2)}) async-start(), calls=%async_computation.10 | async-start | bytes 9437184 | tf_op jit(solution)/shard_map/all_gather | solution.py:23
  415.4 3.2 copy-start.36
  417.2 106.9 %all-gather.14.cloned.1.call-start = ((), (), s32[]{:S(2)}) async-start(), calls=%async_computation.12 | async-start | bytes 1310720 | tf_op jit(solution)/shard_map/all_gather | solution.py:67
  417.8 189.9 %all-gather.16.cloned.1.call-start = ((), (), s32[]{:S(2)}) async-start(), calls=%async_computation.14 | async-start | bytes 9437184 | tf_op jit(solution)/shard_map/all_gather | solution.py:23
  418.5 380.7 %reduce-scatter.13.cloned.1.call-start = ((), (), s32[]{:S(2)}) async-start(), calls=%async_computation.15 | async-start | bytes 18874368 | tf_op jit(solution)/shard_map/reduce_scatter | solution.py:27
  418.6 214.3 %copy-start.34 = (f32[512]{0:T(512)}, f32[512]{0:T(512)S(1)}, u32[]{:S(2)}) copy-start(f32[512]{0:T(512)S(1)} %convert_element_type.106) | copy-start | bytes 6148
  607.7 16.8 copy-start.37
  622.5 2.0 copy-start.39
  632.6 256.9 %reduce-scatter.11.cloned.1.call-start = ((), (), s32[]{:S(2)}) async-start(), calls=%async_computation.13 | async-start | bytes 9437184 | tf_op jit(solution)/shard_map/reduce_scatter | solution.py:127
  645.5 331.1 %all-gather.18.cloned.1.call-start = ((), (), s32[]{:S(2)}) async-start(), calls=%async_computation.16 | async-start | bytes 9437184 | tf_op jit(solution)/shard_map/all_gather | solution.py:23
  889.5 5.1 copy-start.9
  893.3 1.3 copy-start.5
  893.3 1.3 copy-start.22
  895.9 695.2 %reduce-scatter.15.cloned.1.call-start = ((), (), s32[]{:S(2)}) async-start(), calls=%async_computation.17 | async-start | bytes 18874368 | tf_op jit(solution)/shard_map/reduce_scatter | solution.py:27
  992.1 5.7 copy-start
  997.8 7.3 copy-start.3
  1043.9 5.7 copy-start
  1049.7 7.6 copy-start.3
  1096.2 5.7 copy-start
  1101.9 7.6 copy-start.3
  1148.4 5.7 copy-start
  1154.2 7.6 copy-start.3
  1200.7 5.7 copy-start
  1206.4 7.6 copy-start.3
  1252.9 5.7 copy-start
  1258.6 7.6 copy-start.3
  1305.1 5.7 copy-start
  1310.9 7.6 copy-start.3
  1357.4 5.7 copy-start
  1363.1 7.6 copy-start.3
  1424.2 10.9 copy-start.35
  1424.2 211.4 %reduce-scatter.21.cloned.1.call-start = ((), (), s32[]{:S(2)}) async-start(), calls=%async_computation.20 | async-start | bytes 2621440 | tf_op jit(solution)/shard_map/reduce_scatter | solution.py:211
  1434.8 232.5 %reduce-scatter.23.cloned.1.call-start = ((), (), s32[]{:S(2)}) async-start(), calls=%async_computation.21 | async-start | bytes 2621440 | tf_op jit(solution)/shard_map/reduce_scatter | solution.py:210
  1447.1 248.5 %reduce-scatter.19.cloned.1.call-start = ((), (), s32[]{:S(2)}) async-start(), calls=%async_computation.19 | async-start | bytes 655360 | tf_op jit(solution)/shard_map/reduce_scatter | solution.py:209
  1449.2 4.8 copy-start.8
  1459.5 9.2 copy-start.11
  1459.5 270.8 %reduce-scatter.17.cloned.1.call-start = ((), (), s32[]{:S(2)}) async-start(), calls=%async_computation.18 | async-start | bytes 1966080 | tf_op jit(solution)/shard_map/reduce_scatter | solution.py:207
  1468.6 2.4 copy-start.33
  1468.6 122.5 %copy-start.1 = (bf16[512,1024]{1,0:T(8,128)(2,1)S(1)}, bf16[512,1024]{1,0:T(8,128)(2,1)}, u32[]{:S(2)}) copy-start(bf16[512,1024]{1,0:T(8,128)(2,1)} %param.19) | copy-start | bytes 3145732
  1468.6 122.5 %copy-start.16 = (f32[1024]{0:T(1024)S(1)}, f32[1024]{0:T(1024)}, u32[]{:S(2)}) copy-start(f32[1024]{0:T(1024)} %copy-done.15) | copy-start | bytes 12292
  1468.6 122.5 %copy-start.18 = (f32[512]{0:T(512)S(1)}, f32[512]{0:T(512)}, u32[]{:S(2)}) copy-start(f32[512]{0:T(512)} %copy-done.17) | copy-start | bytes 6148
  1468.6 124.8 %copy-start.25 = (f32[512]{0:T(512)S(1)}, f32[512]{0:T(512)}, u32[]{:S(2)}) copy-start(f32[512]{0:T(512)} %copy-done.24) | copy-start | bytes 6148
  1468.7 124.8 %copy-start.21 = (f32[512]{0:T(512)S(1)}, f32[512]{0:T(512)}, u32[]{:S(2)}) copy-start(f32[512]{0:T(512)} %copy-done.20) | copy-start | bytes 6148
  1468.9 125.6 %copy-start.6 = (f32[512,1024]{1,0:T(8,128)S(1)}, f32[512,1024]{1,0:T(8,128)}, u32[]{:S(2)}) copy-start(f32[512,1024]{1,0:T(8,128)} %copy-done.5) | copy-start | bytes 6291460
  1468.9 125.6 %copy-start.23 = (f32[512]{0:T(512)S(1)}, f32[512]{0:T(512)}, u32[]{:S(2)}) copy-start(f32[512]{0:T(512)} %copy-done.22) | copy-start | bytes 6148
  1591.1 2.3 copy-start.4
  1591.1 3.4 copy-start.10
  1594.5 2.3 copy-start.26
  1594.5 2.3 copy-start.27
  (4 other events, 2.8 us)
Sparse Core Ops, SparseCore 0:
  15.5 84.8 all-gather.7
  246.4 166.7 reduce-scatter.8
  896.0 80.5 all-gather.17
  1424.3 166.7 reduce-scatter.14
  1594.5 33.9 reduce-scatter.20
  1632.1 35.1 reduce-scatter.22
  1670.8 24.7 reduce-scatter.18
  1699.4 30.9 reduce-scatter.16
Sparse Core Ops, SparseCore 1:
  248.6 24.8 all-gather.11
  417.3 80.2 all-gather.9
  499.3 24.8 all-gather.13
  525.8 81.9 all-gather.15
  632.7 166.5 reduce-scatter.12
  801.6 87.8 reduce-scatter.10
where the time goes:
time: 1740 us
  waiting for transfers between devices  918 us (53%)
  matrix products  421 us (24%)
  other arithmetic  186 us (11%)
  blocking collectives  85.6 us (5%)
  local copies, waits for them, and re-layouts  82.3 us (5%)
  loops' own time  27.5 us (2%)
    reduce_scatter x2, waiting for transfers between devices, sum_tokens(): lax.psum_scatter(term_fn(jnp.int32(0), lax.axis_size('col') * local_rows)...  263 us
    all_gather x3, waiting for transfers between devices, gather_tokens(): return lax.all_gather(rows_in, 'col', axis=0, tiled=True)  243 us
    reduce_scatter x1, waiting for transfers between devices, body(): lax.psum_scatter(jnp.dot(part, out_weight, preferred_element_type=f32), '...  166 us
    dot_general x8, matrix products, backward_block(): jnp.einsum('qhd,khd->hqk', dout_part, value_seq, preferred_element_type=f32)  101 us
    convert_element_type x8, other arithmetic, backward_block(): d_scores_low = d_scores.astype(bf16)  98.2 us
    reduce_scatter x1, waiting for transfers between devices, body(): lax.psum_scatter(jnp.dot(part, down_all, preferred_element_type=f32).asty...  87.3 us
    dot_general x8, matrix products, backward_block(): jnp.einsum('hqk,qhd->khd', probs_low, dout_part, preferred_element_type=f32)  60.6 us
    dot_general x16, matrix products, block_scores(): jnp.einsum('qhd,khd->hqk', query_part, key_seq, preferred_element_type=f32)  56.1 us
  transfers between devices with their start and end apart: 14, of which 12 were waited for; matrix products, arithmetic and copies ran while one was open for 5% of the time, Pallas kernels for 0%

commit v1 on v0

--- a/solution.py
+++ b/solution.py
@@ -2,6 +2,7 @@
 import jax.numpy as jnp
 from jax import lax
 from jax.sharding import PartitionSpec as P
+from jax.lax import psum
 
 HD = 64
 SEQ_LEN = 4096
@@ -211,8 +212,12 @@
         lax.psum_scatter(grad_wup, "row", scatter_dimension=1, tiled=True),
     )
     grad_bqv, grad_bup = lax.psum((grad_bqv, grad_bup), "row")
-    grad_gain1, grad_shift1, grad_gain2, grad_shift2, grad_bout, grad_bdown = lax.psum(
-        (grad_gain1, grad_shift1, grad_gain2, grad_shift2, grad_bout, grad_bdown), ("row", "col")
+    grad_gain1, grad_shift1, grad_gain2, grad_shift2, grad_bout, grad_bdown = psum(
+        psum(
+            (grad_gain1, grad_shift1, grad_gain2, grad_shift2, grad_bout, grad_bdown),
+            axis_name="col",
+        ),
+        axis_name="row",
     )
     return (
         output,

time: 1740 us -> 1740 us (level)
  no operation moved by 1% of the time
where the time goes in v1:
time: 1740 us
  waiting for transfers between devices  925 us (53%)
  matrix products  421 us (24%)
  other arithmetic  186 us (11%)
  local copies, waits for them, and re-layouts  82.2 us (5%)
  blocking collectives  79.3 us (5%)
  loops' own time  27.5 us (2%)
    reduce_scatter x2, waiting for transfers between devices, sum_tokens(): lax.psum_scatter(term_fn(jnp.int32(0), lax.axis_size('col') * local_rows)...  273 us
    all_gather x3, waiting for transfers between devices, gather_tokens(): return lax.all_gather(rows_in, 'col', axis=0, tiled=True)  243 us
    reduce_scatter x1, waiting for transfers between devices, body(): lax.psum_scatter(jnp.dot(part, out_weight, preferred_element_type=f32), '...  166 us
    dot_general x8, matrix products, backward_block(): jnp.einsum('qhd,khd->hqk', dout_part, value_seq, preferred_element_type=f32)  101 us
    convert_element_type x8, other arithmetic, backward_block(): d_scores_low = d_scores.astype(bf16)  98.2 us
    reduce_scatter x1, waiting for transfers between devices, body(): lax.psum_scatter(jnp.dot(part, down_all, preferred_element_type=f32).asty...  87.3 us
    dot_general x8, matrix products, backward_block(): jnp.einsum('hqk,qhd->khd', probs_low, dout_part, preferred_element_type=f32)  60.6 us
    dot_general x16, matrix products, block_scores(): jnp.einsum('qhd,khd->hqk', query_part, key_seq, preferred_element_type=f32)  56.2 us
  transfers between devices with their start and end apart: 14, of which 12 were waited for; matrix products, arithmetic and copies ran while one was open for 5% of the time, Pallas kernels for 0%

profile of v1, /device:TPU:0, one launch (start us, length us, event | category | flops | bytes accessed | tf_op | source)
XLA Modules:
  0.0 1738.0 jit_solution(1961966382327832416)
XLA Ops:
  15.6 12.7 all_gather.29
  28.6 13.3 all-gather
  41.9 10.6 all_gather.30
  53.5 46.9 %all-gather.8.cloned.1.call-done = bf16[4096,1024]{1,0:T(8,128)(2,1)} async-done(((bf16[512,1024]{1,0:T(8,128)(2,1)}), bf16[4096,1024]{1,0:T(8,128)(2,1)}) %all-gather.8.cloned.1.call-update) | async-done | bytes 8388624 | tf_op jit(solution)/shard_map/all_gather | solution.py:75
  100.4 5.9 fusion.44
  107.3 127.8 %while.29 = (s32[]{:T(128)}, bf16[8,512,2,64]{1,3,2,0:T(8,128)(2,1)}, f32[8,2,512,1]{2,1,3,0:T(2,128)S(1)}, s32[8]{0:T(128)S(1)}, s32[4096]{0:T(1024)S(1)}, /*in...) while((s32[]{:T(128)}, ...), condition=%wide.region_5.6_spmd.clone, body=%wide.region_2.5_spmd.sunk.clone | while | flops 1121975296 | bytes 61266096 | solution.py:108
  238.1 8.1 fusion.77
  247.0 166.2 %reduce-scatter.9.cloned.1.call-done = f32[512,1024]{1,0:T(8,128)} async-done(((f32[4096,1024]{1,0:T(8,128)}), f32[512,1024]{1,0:T(8,128)}) %reduce-scatter.9.cloned.1.call-update) | async-done | bytes 2097168 | tf_op jit(solution)/shard_map/reduce_scatter | solution.py:111
  418.7 78.9 %all-gather.10.cloned.1.call-done = bf16[4096,1024]{1,0:T(8,128)(2,1)} async-done(((bf16[512,1024]{1,0:T(8,128)(2,1)}), bf16[4096,1024]{1,0:T(8,128)(2,1)}) %all-gather.10.cloned.1.call-update) | async-done | bytes 8388624 | tf_op jit(solution)/shard_map/all_gather | solution.py:24
  497.6 11.4 fusion.78
  509.0 15.2 all-gather.14.cloned.1.call-done
  524.1 83.6 %all-gather.16.cloned.1.call-done = bf16[4096,1024]{1,0:T(8,128)(2,1)} async-done(((bf16[512,1024]{1,0:T(8,128)(2,1)}), bf16[4096,1024]{1,0:T(8,128)(2,1)}) %all-gather.16.cloned.1.call-update) | async-done | bytes 8388624 | tf_op jit(solution)/shard_map/all_gather | solution.py:24
  607.7 14.8 fusion.71
  624.5 8.1 fusion.61
  632.9 12.6 convolution_convert_fusion
  646.1 153.2 %reduce-scatter.13.cloned.1.call-done = f32[512,1024]{1,0:T(8,128)} async-done(((f32[4096,1024]{1,0:T(8,128)}), f32[512,1024]{1,0:T(8,128)}) %reduce-scatter.13.cloned.1.call-update) | async-done | bytes 2097168 | tf_op jit(solution)/shard_map/reduce_scatter | solution.py:28
  802.2 87.3 %reduce-scatter.11.cloned.1.call-done = bf16[512,1024]{1,0:T(8,128)(2,1)} async-done(((bf16[4096,1024]{1,0:T(8,128)(2,1)}), bf16[512,1024]{1,0:T(8,128)(2,1)}) %reduce-scatter.11.cloned.1.call-update) | async-done | bytes 1048592 | tf_op jit(solution)/shard_map/reduce_scatter | solution.py:128
  896.0 80.6 %all-gather.18.cloned.1.call-done = bf16[4096,1024]{1,0:T(8,128)(2,1)} async-done(((bf16[512,1024]{1,0:T(8,128)(2,1)}), bf16[4096,1024]{1,0:T(8,128)(2,1)}) %all-gather.18.cloned.1.call-update) | async-done | bytes 8388624 | tf_op jit(solution)/shard_map/all_gather | solution.py:24
  976.6 7.2 convolution_convert_fusion.1
  983.8 418.2 %while.30 = (s32[]{:T(128)}, f32[4096,2,64]{0,2,1:T(8,128)S(1)}, f32[4096,2,64]{0,2,1:T(8,128)}, f32[8,512,2,64]{1,3,2,0:T(8,128)}, s32[8]{0:T(128)S(1)}, /*inde...) while((s32[]{:T(128)}, f32[4096,2,64]{0,2,1:T(8,128)S(1)}, ...), condition=%wide.region_15.16_spmd.clone.clone, body=%wide.region_13.15_spmd.clone.sunk.clone | while | flops 2752052224 | bytes 217893168 | solution.py:189
  992.1 5.7 copy-done
  997.8 7.2 fusion.153
  1005.0 12.7 multiply_reduce_fusion.6
  1017.7 12.3 multiply_convert_fusion.6
  1043.9 5.7 copy-done
  1049.7 7.6 fusion.153
  1057.3 12.6 multiply_reduce_fusion.6
  1069.9 12.3 multiply_convert_fusion.6
  1096.2 5.7 copy-done
  1101.9 7.6 fusion.153
  1109.5 12.7 multiply_reduce_fusion.6
  1122.2 12.3 multiply_convert_fusion.6
  1148.4 5.7 copy-done
  1154.2 7.6 fusion.153
  1161.8 12.6 multiply_reduce_fusion.6
  1174.4 12.3 multiply_convert_fusion.6
  1200.7 5.7 copy-done
  1206.4 7.6 fusion.153
  1214.0 12.6 multiply_reduce_fusion.6
  1226.7 12.3 multiply_convert_fusion.6
  1252.9 5.7 copy-done
  1258.6 7.6 fusion.153
  1266.3 12.7 multiply_reduce_fusion.6
  1278.9 12.3 multiply_convert_fusion.6
  1305.2 5.7 copy-done
  1310.9 7.6 fusion.153
  1318.5 12.7 multiply_reduce_fusion.6
  1331.2 12.3 multiply_convert_fusion.6
  1357.4 5.7 copy-done
  1363.1 7.6 fusion.153
  1370.8 12.7 multiply_reduce_fusion.6
  1383.4 12.3 multiply_convert_fusion.6
  1402.7 6.4 copy.50
  1414.9 9.3 convolution_bitcast_fusion
  1424.2 10.6 fusion.59
  1435.1 12.0 fusion.69
  1453.9 5.5 fusion.79
  1459.6 9.0 fusion.42
  1471.0 120.1 %reduce-scatter.15.cloned.1.call-done = f32[512,1024]{1,0:T(8,128)} async-done(((f32[4096,1024]{1,0:T(8,128)}), f32[512,1024]{1,0:T(8,128)}) %reduce-scatter.15.cloned.1.call-update) | async-done | bytes 2097168 | tf_op jit(solution)/shard_map/reduce_scatter | solution.py:28
  1596.8 26.0 %all-reduce = (f32[1024]{0:T(1024)S(1)}, f32[1024]{0:T(1024)S(1)}, f32[1024]{0:T(1024)S(1)}, f32[1024]{0:T(1024)S(1)}, f32[1024]{0:T(1024)S(1)}, /*index=5*/f32[1024]{0:T(1024)S(1)}) all-reduce(f32[1024]{0:T(1024)S(1)} %get-tuple-element.165, f32[1024]{0:T(1024)S(1)} %get-tuple-element.164, ...), channel_id=1, replica_groups=mesh['row'=4,'col'=8] {'col'}, use_global_device_ids=true, to_apply=%region_25.26 | all-reduce | flops 6144 | bytes 49152 | tf_op jit(solution)/shard_map/psum | solution.py:216
  1622.8 16.8 all-reduce.1
  1639.6 27.8 %reduce-scatter.23.cloned.1.call-done = f32[512,256]{1,0:T(8,128)} async-done(((f32[512,1024]{1,0:T(8,128)}), f32[512,256]{1,0:T(8,128)}) %reduce-scatter.23.cloned.1.call-update) | async-done | bytes 524304 | tf_op jit(solution)/shard_map/reduce_scatter | solution.py:211
  1667.4 28.2 %reduce-scatter.19.cloned.1.call-done = f32[128,256]{1,0:T(8,128)} async-done(((f32[128,1024]{1,0:T(8,128)}), f32[128,256]{1,0:T(8,128)}) %reduce-scatter.19.cloned.1.call-update) | async-done | bytes 131088 | tf_op jit(solution)/shard_map/reduce_scatter | solution.py:210
  1695.6 34.8 %reduce-scatter.17.cloned.1.call-done = f32[256,3,128]{2,0,1:T(8,128)} async-done(((f32[1024,3,128]{2,0,1:T(8,128)}), f32[256,3,128]{2,0,1:T(8,128)}) %reduce-scatter.17.cloned.1.call-update) | async-done | bytes 393232 | tf_op jit(solution)/shard_map/reduce_scatter | solution.py:208
  (296 shorter events, 265.5 us)
Async XLA Ops:
  8.0 7.4 copy-start.38
  8.0 7.6 copy-start.14
  8.0 20.5 %copy-start.28 = (s32[512]{0:T(512)S(1)}, s32[512]{0:T(512)}, u32[]{:S(2)}) copy-start(s32[512]{0:T(512)} %param.20) | copy-start | bytes 6148
  8.0 33.8 %copy-start.19 = (bf16[128,256]{1,0:T(8,128)(2,1)S(1)}, bf16[128,256]{1,0:T(8,128)(2,1)}, u32[]{:S(2)}) copy-start(bf16[128,256]{1,0:T(8,128)(2,1)} %param.23) | copy-start | bytes 196612
  8.1 92.3 %all-gather.8.cloned.1.call-start = ((), (), s32[]{:S(2)}) async-start(), calls=%async_computation.8 | async-start | bytes 9437184 | tf_op jit(solution)/shard_map/all_gather | solution.py:75
  9.6 3.1 copy-start.17
  11.3 4.3 copy-start.24
  11.3 4.3 copy-start.20
  15.3 397.9 %reduce-scatter.9.cloned.1.call-start = ((), (), s32[]{:S(2)}) async-start(), calls=%async_computation.9 | async-start | bytes 18874368 | tf_op jit(solution)/shard_map/reduce_scatter | solution.py:111
  28.3 78.0 %copy-start.12 = (bf16[1024,3,128]{2,0,1:T(8,128)(2,1)}, bf16[1024,3,128]{2,0,1:T(8,128)(2,1)S(1)}, u32[]{:S(2)}) copy-start(bf16[1024,3,128]{2,0,1:T(8,128)(2,1)S(1)} %all_gather.29) | copy-start | bytes 2359300
  235.1 2.6 copy-start.13
  235.2 11.1 copy-start.2
  238.1 8.1 copy-start.7
  246.3 0.7 copy-start.31
  246.3 172.4 %all-gather.12.cloned.1.call-start = ((), (), s32[]{:S(2)}) async-start(), calls=%async_computation.11 | async-start | bytes 1310720 | tf_op jit(solution)/shard_map/all_gather | solution.py:69
  246.9 250.7 %all-gather.10.cloned.1.call-start = ((), (), s32[]{:S(2)}) async-start(), calls=%async_computation.10 | async-start | bytes 9437184 | tf_op jit(solution)/shard_map/all_gather | solution.py:24
  415.4 3.2 copy-start.36
  417.2 106.9 %all-gather.14.cloned.1.call-start = ((), (), s32[]{:S(2)}) async-start(), calls=%async_computation.12 | async-start | bytes 1310720 | tf_op jit(solution)/shard_map/all_gather | solution.py:68
  417.8 189.9 %all-gather.16.cloned.1.call-start = ((), (), s32[]{:S(2)}) async-start(), calls=%async_computation.14 | async-start | bytes 9437184 | tf_op jit(solution)/shard_map/all_gather | solution.py:24
  418.5 380.8 %reduce-scatter.13.cloned.1.call-start = ((), (), s32[]{:S(2)}) async-start(), calls=%async_computation.15 | async-start | bytes 18874368 | tf_op jit(solution)/shard_map/reduce_scatter | solution.py:28
  418.6 214.2 %copy-start.34 = (f32[512]{0:T(512)}, f32[512]{0:T(512)S(1)}, u32[]{:S(2)}) copy-start(f32[512]{0:T(512)S(1)} %convert_element_type.106) | copy-start | bytes 6148
  607.7 16.8 copy-start.37
  622.5 2.0 copy-start.39
  632.6 256.9 %reduce-scatter.11.cloned.1.call-start = ((), (), s32[]{:S(2)}) async-start(), calls=%async_computation.13 | async-start | bytes 9437184 | tf_op jit(solution)/shard_map/reduce_scatter | solution.py:128
  645.4 331.1 %all-gather.18.cloned.1.call-start = ((), (), s32[]{:S(2)}) async-start(), calls=%async_computation.16 | async-start | bytes 9437184 | tf_op jit(solution)/shard_map/all_gather | solution.py:24
  889.5 5.1 copy-start.9
  893.3 1.3 copy-start.5
  893.3 1.3 copy-start.22
  895.9 695.2 %reduce-scatter.15.cloned.1.call-start = ((), (), s32[]{:S(2)}) async-start(), calls=%async_computation.17 | async-start | bytes 18874368 | tf_op jit(solution)/shard_map/reduce_scatter | solution.py:28
  992.1 5.7 copy-start
  997.8 7.3 copy-start.3
  1043.9 5.7 copy-start
  1049.7 7.6 copy-start.3
  1096.2 5.7 copy-start
  1101.9 7.6 copy-start.3
  1148.4 5.7 copy-start
  1154.2 7.6 copy-start.3
  1200.7 5.7 copy-start
  1206.4 7.6 copy-start.3
  1252.9 5.7 copy-start
  1258.6 7.6 copy-start.3
  1305.1 5.7 copy-start
  1310.9 7.6 copy-start.3
  1357.4 5.7 copy-start
  1363.1 7.6 copy-start.3
  1424.2 10.9 copy-start.35
  1424.2 215.4 %reduce-scatter.21.cloned.1.call-start = ((), (), s32[]{:S(2)}) async-start(), calls=%async_computation.20 | async-start | bytes 2621440 | tf_op jit(solution)/shard_map/reduce_scatter | solution.py:212
  1434.8 232.6 %reduce-scatter.23.cloned.1.call-start = ((), (), s32[]{:S(2)}) async-start(), calls=%async_computation.21 | async-start | bytes 2621440 | tf_op jit(solution)/shard_map/reduce_scatter | solution.py:211
  1447.1 248.5 %reduce-scatter.19.cloned.1.call-start = ((), (), s32[]{:S(2)}) async-start(), calls=%async_computation.19 | async-start | bytes 655360 | tf_op jit(solution)/shard_map/reduce_scatter | solution.py:210
  1449.2 4.8 copy-start.8
  1459.5 9.2 copy-start.11
  1459.5 270.8 %reduce-scatter.17.cloned.1.call-start = ((), (), s32[]{:S(2)}) async-start(), calls=%async_computation.18 | async-start | bytes 1966080 | tf_op jit(solution)/shard_map/reduce_scatter | solution.py:208
  1468.6 122.5 %copy-start.1 = (bf16[512,1024]{1,0:T(8,128)(2,1)S(1)}, bf16[512,1024]{1,0:T(8,128)(2,1)}, u32[]{:S(2)}) copy-start(bf16[512,1024]{1,0:T(8,128)(2,1)} %param.19) | copy-start | bytes 3145732
  1468.6 122.5 %copy-start.16 = (f32[1024]{0:T(1024)S(1)}, f32[1024]{0:T(1024)}, u32[]{:S(2)}) copy-start(f32[1024]{0:T(1024)} %copy-done.15) | copy-start | bytes 12292
  1468.6 122.5 %copy-start.18 = (f32[512]{0:T(512)S(1)}, f32[512]{0:T(512)}, u32[]{:S(2)}) copy-start(f32[512]{0:T(512)} %copy-done.17) | copy-start | bytes 6148
  1468.6 124.8 %copy-start.25 = (f32[512]{0:T(512)S(1)}, f32[512]{0:T(512)}, u32[]{:S(2)}) copy-start(f32[512]{0:T(512)} %copy-done.24) | copy-start | bytes 6148
  1468.6 124.8 %copy-start.21 = (f32[512]{0:T(512)S(1)}, f32[512]{0:T(512)}, u32[]{:S(2)}) copy-start(f32[512]{0:T(512)} %copy-done.20) | copy-start | bytes 6148
  1468.9 125.6 %copy-start.6 = (f32[512,1024]{1,0:T(8,128)S(1)}, f32[512,1024]{1,0:T(8,128)}, u32[]{:S(2)}) copy-start(f32[512,1024]{1,0:T(8,128)} %copy-done.5) | copy-start | bytes 6291460
  1468.9 125.6 %copy-start.23 = (f32[512]{0:T(512)S(1)}, f32[512]{0:T(512)}, u32[]{:S(2)}) copy-start(f32[512]{0:T(512)} %copy-done.22) | copy-start | bytes 6148
  1591.1 2.3 copy-start.4
  1591.1 3.4 copy-start.10
  1594.5 2.3 copy-start.26
  1594.5 2.3 copy-start.27
  1594.5 28.3 %copy-start.33 = (f32[512]{0:T(512)S(1)}, f32[512]{0:T(512)}, u32[]{:S(2)}) copy-start(f32[512]{0:T(512)} %get-tuple-element.222) | copy-start | bytes 6148
  (4 other events, 2.8 us)
Sparse Core Ops, SparseCore 0:
  15.5 84.8 all-gather.7
  246.4 166.7 reduce-scatter.8
  896.0 80.4 all-gather.17
  1424.3 166.7 reduce-scatter.14
  1594.5 33.7 reduce-scatter.20
  1631.9 35.4 reduce-scatter.22
  1670.8 24.7 reduce-scatter.18
  1699.4 30.9 reduce-scatter.16
Sparse Core Ops, SparseCore 1:
  248.6 24.8 all-gather.11
  417.3 80.2 all-gather.9
  499.3 24.8 all-gather.13
  525.8 81.9 all-gather.15
  632.7 166.6 reduce-scatter.12
  801.6 87.8 reduce-scatter.10
